TPU v7x, 32 devices: a whole 2x2x4 slice. The times are simulated.
32 devices in a mesh: ep: 8 (over z, x), tp: 4 (over y, core).
Axes of the slice: x: 2, y: 2, z: 4, core: 2. Of those that a mesh axis runs over, the one named last changes fastest.
Arguments:
- tokens: bfloat16 [2, 1024, 4096], P(None, 'ep', 'tp'), may hold values from -6 to 6
- expert_ids: int32 [2, 1024, 8], P(None, 'ep'), may hold values from 0 to 31, all different within a row; in each aligned block of 128 rows (0 to 127, 128 to 255, ..., all dimensions but the last counted through in order) at most 40 rows name the same one
- route_weight: float32 [2, 1024, 8], P(None, 'ep'), may hold values from 0.1 to 1
- gate_weight: bfloat16 [32, 1536, 4096], P('ep', 'tp'), may hold values from -0.09375 to 0.09375
- up_weight: bfloat16 [32, 1536, 4096], P('ep', 'tp'), may hold values from -0.09375 to 0.09375
- down_weight: bfloat16 [32, 1536, 4096], P('ep', None, 'tp'), may hold values from -0.15625 to 0.15625
- home_slot: int32 [32], replicated, may hold values from 0 to 31, as said below
- spare_expert: int32 [8], replicated, may hold values from 0 to 31, as said below
Outputs:
- mixed: bfloat16 [2, 1024, 4096], P(None, 'ep', 'tp')
- spare_gate: bfloat16 [8, 1536, 4096], P('ep', 'tp')
- spare_up: bfloat16 [8, 1536, 4096], P('ep', 'tp')
- spare_down: bfloat16 [8, 1536, 4096], P('ep', None, 'tp')
Inputs may be any that keep to these rules, and one draw needn't show every extreme that they name: `home_slot`: a permutation; slot s belongs to ep index s // 4. `spare_expert`: names at most 6 distinct experts, whose home slots lie on distinct ep indices; entry d never names an expert whose home slot lies on ep index d. `expert_ids`: each token names 8 distinct experts; in each micro-step the 128 tokens of one ep index name one expert at most 40 times.
All inputs are finite; a program needn't handle non-finite values.
Results may differ from a plain program's by a relative error of at most 0.0058.
Values may be sent and summed in bfloat16 or wider, within the bound.
No kernel may reach another device: no remote copies, remote signals or barrier semaphores. Data moves between devices by JAX's collectives and lax.ppermute only.
A program may use at most 192 MiB of HBM per device.

v0:
```python
import jax
import jax.numpy as jnp
from jax import lax
from jax.sharding import PartitionSpec as P

TOP = 8
STEPS = 2


def slot_targets(expert_pick, home_slot, capacity):
    count_all = home_slot.shape[0]
    expert_iota = lax.iota(jnp.int32, count_all)
    slot_pick = jnp.sum(jnp.where(expert_pick[..., None] == expert_iota, home_slot, 0), axis=-1)
    pair_shape = expert_pick.shape[:-2] + (expert_pick.shape[-2] * expert_pick.shape[-1],)
    pair_slot = slot_pick.reshape(pair_shape)
    one_hot = (pair_slot[..., None] == expert_iota).astype(jnp.int32)
    earlier = jnp.cumsum(one_hot, axis=-2) - one_hot
    position = jnp.sum(earlier * one_hot, axis=-1)
    return (pair_slot * capacity + position).reshape(expert_pick.shape)


def run_steps(tokens, expert_pick, route_weight, gate_weight, up_weight, down_weight, home_slot):
    batches = tokens.shape[0]
    tok_count = tokens.shape[1]
    width_local = tokens.shape[2]
    experts_all = home_slot.shape[0]
    local_count = gate_weight.shape[0]
    owners = experts_all // local_count
    capacity = tok_count * TOP * 5 // (4 * experts_all)
    slot_rows = local_count * capacity
    total_rows = experts_all * capacity
    own_target = slot_targets(expert_pick, home_slot, capacity)
    placing = jnp.any(own_target[..., None] == lax.iota(jnp.int32, total_rows), axis=2).astype(
        jnp.bfloat16
    )
    outgoing = jnp.einsum(
        "btr,btd->brd", placing, tokens, preferred_element_type=jnp.float32
    ).astype(jnp.bfloat16)
    outgoing = outgoing.reshape(batches, owners, slot_rows, width_local)
    arrived = lax.all_to_all(outgoing, "ep", split_axis=1, concat_axis=1, tiled=True)
    piece = lax.all_gather(arrived, "tp", axis=3, tiled=True)
    piece_rows = piece.reshape(batches, owners, local_count, capacity, piece.shape[3])
    gate_add = jnp.einsum(
        "bsecd,efd->bsecf", piece_rows, gate_weight, preferred_element_type=jnp.float32
    )
    up_add = jnp.einsum(
        "bsecd,efd->bsecf", piece_rows, up_weight, preferred_element_type=jnp.float32
    )
    hidden = (jax.nn.silu(gate_add) * up_add).astype(jnp.bfloat16)
    results = jnp.einsum(
        "bsecf,efd->bsecd",
        lax.all_gather(hidden, "tp", axis=4, tiled=True),
        down_weight,
        preferred_element_type=jnp.float32,
    ).astype(jnp.bfloat16)
    results = results.reshape(batches, owners, slot_rows, width_local)
    returned = lax.all_to_all(results, "ep", split_axis=1, concat_axis=1, tiled=True)
    returned = returned.reshape(batches, total_rows, width_local)
    flat_target = own_target.reshape(batches, tok_count * own_target.shape[2])
    picked_rows = jnp.take_along_axis(returned, flat_target[..., None], axis=1)
    picked_rows = picked_rows.reshape(batches, tok_count, own_target.shape[2], width_local).astype(
        jnp.float32
    )
    mixed = jnp.sum(picked_rows * route_weight[..., None], axis=2)
    return mixed.astype(jnp.bfloat16)


def move_spares(gate_weight, up_weight, down_weight, home_slot, spare_expert):
    local_count = gate_weight.shape[0]
    experts_all = home_slot.shape[0]
    owners = spare_expert.shape[0]
    own_index = lax.axis_index("ep")
    expert_iota = lax.iota(jnp.int32, experts_all)
    spare_slot = jnp.sum(jnp.where(spare_expert[:, None] == expert_iota, home_slot, 0), axis=1)
    spare_home = spare_slot // local_count
    own_slot = jnp.max(jnp.where(spare_home == own_index, spare_slot % local_count, 0))
    gate_part = lax.dynamic_index_in_dim(gate_weight, own_slot, 0, keepdims=False)
    up_part = lax.dynamic_index_in_dim(up_weight, own_slot, 0, keepdims=False)
    down_part = lax.dynamic_index_in_dim(down_weight, own_slot, 0, keepdims=False)
    gate_pieces = gate_part.reshape(gate_part.shape[0], owners, gate_part.shape[1] // owners)
    up_pieces = up_part.reshape(up_part.shape[0], owners, up_part.shape[1] // owners)
    down_pieces = down_part.reshape(down_part.shape[0], owners, down_part.shape[1] // owners)
    spread_gate, spread_up, spread_down = (
        lax.all_to_all(gate_pieces, "ep", split_axis=1, concat_axis=1, tiled=True),
        lax.all_to_all(up_pieces, "ep", split_axis=1, concat_axis=1, tiled=True),
        lax.all_to_all(down_pieces, "ep", split_axis=1, concat_axis=1, tiled=True),
    )
    chosen_gate = jnp.take(spread_gate, spare_home, axis=1)
    chosen_up = jnp.take(spread_up, spare_home, axis=1)
    chosen_down = jnp.take(spread_down, spare_home, axis=1)
    landed_gate, landed_up, landed_down = (
        lax.all_to_all(chosen_gate, "ep", split_axis=1, concat_axis=1, tiled=True),
        lax.all_to_all(chosen_up, "ep", split_axis=1, concat_axis=1, tiled=True),
        lax.all_to_all(chosen_down, "ep", split_axis=1, concat_axis=1, tiled=True),
    )
    spare_gate = landed_gate.reshape(1, gate_part.shape[0], gate_part.shape[1])
    spare_up = landed_up.reshape(1, up_part.shape[0], up_part.shape[1])
    spare_down = landed_down.reshape(1, down_part.shape[0], down_part.shape[1])
    return (spare_gate, spare_up, spare_down)


def shards(
    tokens, expert_ids, route_weight, gate_weight, up_weight, down_weight, home_slot, spare_expert
):
    spare_gate, spare_up, spare_down = move_spares(
        gate_weight, up_weight, down_weight, home_slot, spare_expert
    )
    outputs = [
        run_steps(
            tokens[step_index : step_index + 1],
            expert_ids[step_index : step_index + 1],
            route_weight[step_index : step_index + 1],
            gate_weight,
            up_weight,
            down_weight,
            home_slot,
        )
        for step_index in range(STEPS)
    ]
    mixed = jnp.concatenate(outputs, axis=0)
    return (mixed, spare_gate, spare_up, spare_down)


def solution(mesh):
    placed = (
        P(None, "ep", "tp"),
        P(None, "ep", None),
        P(None, "ep", None),
        P("ep", "tp", None),
        P("ep", "tp", None),
        P("ep", None, "tp"),
        P(),
        P(),
    )
    return jax.shard_map(
        shards,
        mesh=mesh,
        in_specs=placed,
        out_specs=(
            P(None, "ep", "tp"),
            P("ep", "tp", None),
            P("ep", "tp", None),
            P("ep", None, "tp"),
        ),
        check_vma=False,
    )
```

profile of v0, /device:TPU:0, one launch (start us, length us, event | category | flops | bytes accessed | tf_op | source)
XLA Modules:
  0.0 761.4 jit_solution(297695629966626307)
XLA Ops:
  9.0 9.0 %reduce-window.14 = s32[1,32,8,128]{3,2,1,0:T(8,128)S(1)} reduce-window(s32[1,32,8,128]{3,2,1,0:T(8,128)S(1)} %bitcast.226, s32[]{:T(128)} %constant.82.clone.1), window={size=1x1x1x128 pad=0_0x0_0x0_0x127_0}, to_apply=%region_1.2 | reduce-window | flops 4161536 | bytes 262148 | tf_op jit(solution)/shard_map/reduce-window
  18.4 9.0 %reduce-window.16 = s32[1,32,8,128]{3,2,1,0:T(8,128)S(1)} reduce-window(s32[1,32,8,128]{3,2,1,0:T(8,128)S(1)} %bitcast.227, s32[]{:T(128)} %constant.82.clone.1), window={size=1x1x1x128 pad=0_0x0_0x0_0x127_0}, to_apply=%region_7.9 | reduce-window | flops 4161536 | bytes 262148 | tf_op jit(solution)/shard_map/reduce-window.2
  31.4 66.7 %all_to_all.50 = bf16[1,8,160,1024]{3,2,0,1:T(8,128)(2,1)} all-to-all(bf16[1,8,160,1024]{3,2,0,1:T(8,128)(2,1)S(1)} %bitcast.223), channel_id=1, replica_groups=mesh['ep'=8,'tp'=4] {'ep'}, dimensions={1} | all-to-all | bytes 5242880 | tf_op jit(solution)/shard_map/all_to_all | solution.py:40
  102.2 4.6 all-to-all-start.2
  109.7 6.8 constant_dynamic-slice_fusion.1
  122.7 42.7 %all-to-all-done.2 = bf16[1,8,160,1024]{3,2,0,1:T(8,128)(2,1)} async-done(((bf16[1,8,160,1024]{3,2,0,1:T(8,128)(2,1)}), bf16[1,8,160,1024]{3,2,0,1:T(8,128)(2,1)}, u32[]{:S(2)}, u32[]{:S(2)}) %all-to-all-start.2) | async-done | bytes 2621472 | tf_op jit(solution)/shard_map/all_to_all | solution.py:40
  169.0 4.6 copy.130
  173.7 4.6 copy.118
  178.3 61.6 %all-to-all-done.4 = bf16[384,8,512]{2,0,1:T(8,128)(2,1)S(1)} async-done(((bf16[384,8,512]{2,0,1:T(8,128)(2,1)}), bf16[384,8,512]{2,0,1:T(8,128)(2,1)S(1)}, u32[]{:S(2)}, u32[]{:S(2)}) %all-to-all-start.4) | async-done | bytes 3145760 | tf_op jit(solution)/shard_map/all_to_all | solution.py:84
  251.9 4.6 copy.121
  256.5 59.7 %all-to-all-done.6 = bf16[384,8,512]{2,0,1:T(8,128)(2,1)} async-done(((bf16[384,8,512]{2,0,1:T(8,128)(2,1)}), bf16[384,8,512]{2,0,1:T(8,128)(2,1)}, u32[]{:S(2)}, u32[]{:S(2)}) %all-to-all-start.6) | async-done | bytes 3145760 | tf_op jit(solution)/shard_map/all_to_all | solution.py:85
  328.5 6.2 select_bitcast_fusion
  334.6 56.1 %all-to-all-done.8 = bf16[1536,8,128]{2,0,1:T(8,128)(2,1)S(1)} async-done(((bf16[1536,8,128]{2,0,1:T(8,128)(2,1)}), bf16[1536,8,128]{2,0,1:T(8,128)(2,1)S(1)}, u32[]{:S(2)}, u32[]{:S(2)}) %all-to-all-start.8) | async-done | bytes 3145760 | tf_op jit(solution)/shard_map/all_to_all | solution.py:86
  390.7 74.8 %all_to_all.51 = bf16[384,8,512]{2,0,1:T(8,128)(2,1)} all-to-all(bf16[384,8,512]{2,0,1:T(8,128)(2,1)} %get-tuple-element.35), channel_id=1, replica_groups=mesh['ep'=8,'tp'=4] {'ep'}, dimensions={1} | all-to-all | bytes 6291456 | tf_op jit(solution)/shard_map/all_to_all | solution.py:92
  469.7 15.1 %fusion.10 = f32[4,8,40,384]{3,2,1,0:T(8,128)} fusion(bf16[4,384,4096]{2,1,0:T(8,128)(2,1)} %param.15, bf16[8,4,40,4096]{3,2,1,0:T(8,128)(2,1)} %bitcast.234), kind=kOutput, calls=%fused_computation.15 | convolution fusion | flops 4026531840 | bytes 25034752 | tf_op jit(solution)/shard_map/bsecd,efd->bsecf/dot_general | solution.py:43
  484.8 15.3 %fusion.31 = bf16[1,8,4,40,384]{4,3,1,2,0:T(8,128)(2,1)} fusion(f32[4,8,40,384]{3,2,1,0:T(8,128)} %fusion.10, bf16[4,384,4096]{2,1,0:T(8,128)(2,1)} %param.16, bf16[8,4,40,4096]{3,2,1,0:T(8,128)(2,1)} %bitcast.235), kind=kOutput, calls=%fused_computation.43 | convolution fusion | flops 4029480960 | bytes 26017792 | tf_op jit(solution)/shard_map/bsecd,efd->bsecf/dot_general | solution.py:46
  508.6 30.7 %all-to-all-done.7 = bf16[384,8,512]{2,0,1:T(8,128)(2,1)S(1)} async-done(((bf16[384,8,512]{2,0,1:T(8,128)(2,1)}), bf16[384,8,512]{2,0,1:T(8,128)(2,1)S(1)}, u32[]{:S(2)}, u32[]{:S(2)}) %all-to-all-start.7) | async-done | bytes 3145760 | tf_op jit(solution)/shard_map/all_to_all | solution.py:93
  545.6 14.2 %fusion.8 = f32[4,8,40,384]{3,2,1,0:T(8,128)S(1)} fusion(bf16[4,384,4096]{2,1,0:T(8,128)(2,1)} %param.15, bf16[8,4,40,4096]{3,2,1,0:T(8,128)(2,1)} %bitcast.236), kind=kOutput, calls=%fused_computation.13 | convolution fusion | flops 4026531840 | bytes 25034752 | tf_op jit(solution)/shard_map/bsecd,efd->bsecf/dot_general | solution.py:43
  559.8 15.0 %fusion.30 = bf16[1,8,4,40,384]{4,3,1,2,0:T(8,128)(2,1)} fusion(f32[4,8,40,384]{3,2,1,0:T(8,128)S(1)} %fusion.8, bf16[4,384,4096]{2,1,0:T(8,128)(2,1)} %param.16, bf16[8,4,40,4096]{3,2,1,0:T(8,128)(2,1)} %bitcast.237), kind=kOutput, calls=%fused_computation.41 | convolution fusion | flops 4029480960 | bytes 26017792 | tf_op jit(solution)/shard_map/bsecd,efd->bsecf/dot_general | solution.py:46
  574.9 10.0 %convert_bitcast_fusion.1 = bf16[1,8,4,40,1024]{4,3,1,2,0:T(8,128)(2,1)S(1)} fusion(bf16[4,1536,1024]{2,1,0:T(8,128)(2,1)} %param.17, bf16[1,8,4,40,1536]{4,3,1,2,0:T(8,128)(2,1)} %all-gather.7.cloned.1.call-done), kind=kOutput, calls=%fused_computation.37 | convolution fusion | flops 4027842560 | bytes 19136512 | tf_op jit(solution)/shard_map/bsecf,efd->bsecd/dot_general | solution.py:50
  586.7 28.9 %all-to-all-done.9 = bf16[1536,8,128]{2,0,1:T(8,128)(2,1)} async-done(((bf16[1536,8,128]{2,0,1:T(8,128)(2,1)}), bf16[1536,8,128]{2,0,1:T(8,128)(2,1)}, u32[]{:S(2)}, u32[]{:S(2)}) %all-to-all-start.9) | async-done | bytes 3145760 | tf_op jit(solution)/shard_map/all_to_all | solution.py:94
  619.5 10.0 %convert_bitcast_fusion = bf16[1,8,4,40,1024]{4,3,1,2,0:T(8,128)(2,1)S(1)} fusion(bf16[4,1536,1024]{2,1,0:T(8,128)(2,1)} %param.17, bf16[1,8,4,40,1536]{4,3,1,2,0:T(8,128)(2,1)} %all-gather.11.cloned.1.call-done), kind=kOutput, calls=%fused_computation.36 | convolution fusion | flops 4027842560 | bytes 19136512 | tf_op jit(solution)/shard_map/bsecf,efd->bsecd/dot_general | solution.py:50
  631.3 47.8 %all-to-all-done.1 = bf16[1,8,160,1024]{3,2,0,1:T(8,128)(2,1)S(1)} async-done(((bf16[1,8,160,1024]{3,2,0,1:T(8,128)(2,1)}), bf16[1,8,160,1024]{3,2,0,1:T(8,128)(2,1)S(1)}, u32[]{:S(2)}, u32[]{:S(2)}) %all-to-all-start.1) | async-done | bytes 2621472 | tf_op jit(solution)/shard_map/all_to_all | solution.py:57
  684.1 4.6 copy.116
  688.8 4.6 copy.123
  693.4 4.6 copy.119
  698.0 4.6 copy.124
  702.7 4.6 copy.122
  707.3 4.6 copy.125
  711.9 5.4 gather_fusion.1
  717.3 25.1 %all-to-all-done.3 = bf16[1,8,160,1024]{3,2,0,1:T(8,128)(2,1)} async-done(((bf16[1,8,160,1024]{3,2,0,1:T(8,128)(2,1)}), bf16[1,8,160,1024]{3,2,0,1:T(8,128)(2,1)}, u32[]{:S(2)}, u32[]{:S(2)}) %all-to-all-start.3) | async-done | bytes 2621472 | tf_op jit(solution)/shard_map/all_to_all | solution.py:57
  742.4 8.2 %gather_fusion.2 = bf16[1024,1024]{1,0:T(8,128)(2,1)} fusion(bf16[1280,1024]{1,0:T(8,128)(2,1)} %bitcast.67, s32[1024]{0:T(1024)S(1)} %broadcast_clamp_fusion), kind=kCustom, calls=%fused_computation.2.clone | custom fusion | bytes 4198400 | tf_op jit(solution)/shard_map/jit(take_along_axis)/gather | solution.py:60
  (106 shorter events, 80.7 us)
Async XLA Ops:
  7.2 23.3 %copy-start.5 = (bf16[2,128,1024]{2,1,0:T(8,128)(2,1)S(1)}, bf16[2,128,1024]{2,1,0:T(8,128)(2,1)}, u32[]{:S(2)}) copy-start(bf16[2,128,1024]{2,1,0:T(8,128)(2,1)} %param.12) | copy-start | bytes 1572868
  7.2 462.5 %all-gather.5.cloned.1.call-start = ((), (), s32[]{:S(2)}) async-start(), calls=%async_computation.10 | async-start | bytes 13107200 | tf_op jit(solution)/shard_map/all_gather | solution.py:41
  102.2 4.6 copy-start.7
  102.2 4.6 copy-start.8
  102.2 63.2 %all-to-all-start.2 = ((bf16[1,8,160,1024]{3,2,0,1:T(8,128)(2,1)}), bf16[1,8,160,1024]{3,2,0,1:T(8,128)(2,1)}, u32[]{:S(2)}, u32[]{:S(2)}) async-start(bf16[1,8,160,1024]{3,2,0,1:T(8,128)(2,1)} %bitcast.46), calls=%async_computation.2 | async-start | bytes 5242880 | tf_op jit(solution)/shard_map/all_to_all | solution.py:40
  165.4 74.5 %all-to-all-start.4 = ((bf16[384,8,512]{2,0,1:T(8,128)(2,1)}), bf16[384,8,512]{2,0,1:T(8,128)(2,1)S(1)}, u32[]{:S(2)}, u32[]{:S(2)}) async-start(bf16[384,8,512]{2,0,1:T(8,128)(2,1)} %copy.115), calls=%async_computation.4 | async-start | bytes 6291456 | tf_op jit(solution)/shard_map/all_to_all | solution.py:84
  239.9 1.7 copy-start.2
  241.6 74.6 %all-to-all-start.6 = ((bf16[384,8,512]{2,0,1:T(8,128)(2,1)}), bf16[384,8,512]{2,0,1:T(8,128)(2,1)}, u32[]{:S(2)}, u32[]{:S(2)}) async-start(bf16[384,8,512]{2,0,1:T(8,128)(2,1)} %copy.118), calls=%async_computation.6 | async-start | bytes 6291456 | tf_op jit(solution)/shard_map/all_to_all | solution.py:85
  246.0 299.6 %all-gather.9.cloned.1.call-start = ((), (), s32[]{:S(2)}) async-start(), calls=%async_computation.12 | async-start | bytes 13107200 | tf_op jit(solution)/shard_map/all_gather | solution.py:41
  316.2 74.5 %all-to-all-start.8 = ((bf16[1536,8,128]{2,0,1:T(8,128)(2,1)}), bf16[1536,8,128]{2,0,1:T(8,128)(2,1)S(1)}, u32[]{:S(2)}, u32[]{:S(2)}) async-start(bf16[1536,8,128]{2,0,1:T(8,128)(2,1)} %copy.121), calls=%async_computation.8 | async-start | bytes 6291456 | tf_op jit(solution)/shard_map/all_to_all | solution.py:86
  390.7 74.8 %copy-start.1 = (bf16[1536,8,128]{2,0,1:T(8,128)(2,1)}, bf16[1536,8,128]{2,0,1:T(8,128)(2,1)S(1)}, u32[]{:S(2)}) copy-start(bf16[1536,8,128]{2,0,1:T(8,128)(2,1)S(1)} %all-to-all-done.8) | copy-start | bytes 9437188
  465.5 73.8 %all-to-all-start.7 = ((bf16[384,8,512]{2,0,1:T(8,128)(2,1)}), bf16[384,8,512]{2,0,1:T(8,128)(2,1)S(1)}, u32[]{:S(2)}, u32[]{:S(2)}) async-start(bf16[384,8,512]{2,0,1:T(8,128)(2,1)} %get-tuple-element.34), calls=%async_computation.7 | async-start | bytes 6291456 | tf_op jit(solution)/shard_map/all_to_all | solution.py:93
  469.2 105.7 %all-gather.7.cloned.1.call-start = ((), (), s32[]{:S(2)}) async-start(), calls=%async_computation.11 | async-start | bytes 4915200 | tf_op jit(solution)/shard_map/all_gather | solution.py:52
  539.2 1.7 copy-start
  540.9 74.6 %all-to-all-start.9 = ((bf16[1536,8,128]{2,0,1:T(8,128)(2,1)}), bf16[1536,8,128]{2,0,1:T(8,128)(2,1)}, u32[]{:S(2)}, u32[]{:S(2)}) async-start(bf16[1536,8,128]{2,0,1:T(8,128)(2,1)} %select_bitcast_fusion.2), calls=%async_computation.9 | async-start | bytes 6291456 | tf_op jit(solution)/shard_map/all_to_all | solution.py:94
  545.4 74.1 %all-gather.11.cloned.1.call-start = ((), (), s32[]{:S(2)}) async-start(), calls=%async_computation.13 | async-start | bytes 4915200 | tf_op jit(solution)/shard_map/all_gather | solution.py:52
  615.6 63.5 %all-to-all-start.1 = ((bf16[1,8,160,1024]{3,2,0,1:T(8,128)(2,1)}), bf16[1,8,160,1024]{3,2,0,1:T(8,128)(2,1)S(1)}, u32[]{:S(2)}, u32[]{:S(2)}) async-start(bf16[1,8,160,1024]{3,2,0,1:T(8,128)(2,1)} %bitcast.222), calls=%async_computation.1 | async-start | bytes 5242880 | tf_op jit(solution)/shard_map/all_to_all | solution.py:57
  631.3 52.4 %copy-start.6 = (f32[2,128,8]{1,2,0:T(8,128)S(1)}, f32[2,128,8]{1,2,0:T(8,128)}, u32[]{:S(2)}) copy-start(f32[2,128,8]{1,2,0:T(8,128)} %param.14) | copy-start | bytes 24580
  679.0 63.4 %all-to-all-start.3 = ((bf16[1,8,160,1024]{3,2,0,1:T(8,128)(2,1)}), bf16[1,8,160,1024]{3,2,0,1:T(8,128)(2,1)}, u32[]{:S(2)}, u32[]{:S(2)}) async-start(bf16[1,8,160,1024]{3,2,0,1:T(8,128)(2,1)} %bitcast.221), calls=%async_computation.3 | async-start | bytes 5242880 | tf_op jit(solution)/shard_map/all_to_all | solution.py:57
  742.4 8.2 %copy-start.3 = (bf16[1024,1024]{1,0:T(8,128)(2,1)S(1)}, bf16[1024,1024]{1,0:T(8,128)(2,1)}, u32[]{:S(2)}) copy-start(bf16[1024,1024]{1,0:T(8,128)(2,1)} %gather_fusion.1) | copy-start | bytes 6291460
  750.7 1.6 copy-start.4
Sparse Core Ops, SparseCore 0:
  98.2 69.1 all-gather.4
  248.4 71.4 all-gather.8
  500.2 34.2 all-gather.6
  575.0 34.2 all-gather.10
where the time goes:
time: 771 us; the launch traced here: 761 us
  waiting for transfers between devices  353 us (46%)
  blocking collectives  141 us (18%)
  local copies, waits for them, and re-layouts  96.8 us (13%)
  matrix products  82.9 us (11%)
  other arithmetic  37.1 us (5%)
  starting transfers between devices  33.5 us (4%)
  between operations  16.4 us (2%)
    all_to_all x1, blocking collectives, move_spares(): lax.all_to_all(chosen_gate, 'ep', split_axis=1, concat_axis=1, tiled=True)  74.8 us
    all_to_all x2, waiting for transfers between devices, run_steps(): lax.all_to_all(results, 'ep', split_axis=1, concat_axis=1, tiled=True)  72.9 us
    all_to_all x1, blocking collectives, run_steps(): lax.all_to_all(outgoing, 'ep', split_axis=1, concat_axis=1, tiled=True)  66.7 us
    all_to_all x1, waiting for transfers between devices, move_spares(): lax.all_to_all(gate_pieces, 'ep', split_axis=1, concat_axis=1, tiled=True)  61.6 us
    all_to_all x1, waiting for transfers between devices, move_spares(): lax.all_to_all(up_pieces, 'ep', split_axis=1, concat_axis=1, tiled=True)  59.7 us
    all_to_all x1, waiting for transfers between devices, move_spares(): lax.all_to_all(down_pieces, 'ep', split_axis=1, concat_axis=1, tiled=True)  56.1 us
    all_to_all x1, waiting for transfers between devices, run_steps(): lax.all_to_all(outgoing, 'ep', split_axis=1, concat_axis=1, tiled=True)  42.7 us
    all_to_all x1, waiting for transfers between devices, move_spares(): lax.all_to_all(chosen_up, 'ep', split_axis=1, concat_axis=1, tiled=True)  30.7 us
  transfers between devices with their start and end apart: 12, of which 8 were waited for; matrix products, arithmetic and copies ran while one was open for 23% of the time, Pallas kernels for 0%

commit v1 on v0

--- a/solution.py
+++ b/solution.py
@@ -1,3 +1,4 @@
+import functools
 import jax
 import jax.numpy as jnp
 from jax import lax
@@ -5,6 +6,36 @@
 
 TOP = 8
 STEPS = 2
+
+
+def point_flows_now(payload, dim_at, z):
+    p_next, lower = (payload.shape[:dim_at], payload.shape[dim_at + 1 :])
+    z_new = payload.reshape(*p_next, z, -1, *lower)
+    return jnp.moveaxis(z_new, dim_at, 0)
+
+
+def guide_digits(s0, array_axis):
+    mat_out = list(s0.shape[1:])
+    mat_out[array_axis] *= s0.shape[0]
+    return jnp.moveaxis(s0, 0, array_axis).reshape(mat_out)
+
+
+def update_the_lots_all(array_in, row_axis, x0, arr):
+    oldest = lax.axis_size(row_axis)
+    fresh = lax.axis_index(row_axis)
+    piece_now, prior = (oldest, fresh)
+    vec_out = point_flows_now(array_in, x0, piece_now)
+    arrivals = [vec_out[prior]]
+    for t in range(1, piece_now):
+        current_block = vec_out[prior ^ t]
+        n_now = lax.ppermute(current_block, row_axis, [(ii, ii ^ t) for ii in range(piece_now)])
+        arrivals.append(n_now)
+    raw_out = jnp.stack(arrivals)
+    vec_out = raw_out[prior ^ jnp.arange(piece_now)]
+    return guide_digits(vec_out, arr)
+
+
+_build_pools = functools.partial(update_the_lots_all, row_axis="ep", x0=1, arr=1)
 
 
 def slot_targets(expert_pick, home_slot, capacity):
@@ -89,7 +120,7 @@
     chosen_up = jnp.take(spread_up, spare_home, axis=1)
     chosen_down = jnp.take(spread_down, spare_home, axis=1)
     landed_gate, landed_up, landed_down = (
-        lax.all_to_all(chosen_gate, "ep", split_axis=1, concat_axis=1, tiled=True),
+        _build_pools(chosen_gate),
         lax.all_to_all(chosen_up, "ep", split_axis=1, concat_axis=1, tiled=True),
         lax.all_to_all(chosen_down, "ep", split_axis=1, concat_axis=1, tiled=True),
     )

time: 771 us -> 803 us (1.042)
  the two profiles are of different devices: /device:TPU:0 before, /device:TPU:8 now
where the time goes in v1:
time: 803 us; the launch traced here: 793 us
  waiting for transfers between devices  408 us (51%)
  local copies, waits for them, and re-layouts  115 us (14%)
  matrix products  82.9 us (10%)
  starting transfers between devices  68.2 us (8%)
  blocking collectives  64.7 us (8%)
  other arithmetic  38.2 us (5%)
  between operations  16.4 us (2%)
    ppermute x7, waiting for transfers between devices, update_the_lots_all(): lax.ppermute(current_block, row_axis, [(ii, ii ^ t) for ii in range(piece...  95.9 us
    all_to_all x1, blocking collectives, run_steps(): lax.all_to_all(outgoing, 'ep', split_axis=1, concat_axis=1, tiled=True)  64.7 us
    all_to_all x1, waiting for transfers between devices, move_spares(): lax.all_to_all(up_pieces, 'ep', split_axis=1, concat_axis=1, tiled=True)  58.4 us
    all_to_all x1, waiting for transfers between devices, move_spares(): lax.all_to_all(gate_pieces, 'ep', split_axis=1, concat_axis=1, tiled=True)  58 us
    all_to_all x1, waiting for transfers between devices, move_spares(): lax.all_to_all(down_pieces, 'ep', split_axis=1, concat_axis=1, tiled=True)  53.7 us
    all_to_all x2, waiting for transfers between devices, run_steps(): lax.all_to_all(results, 'ep', split_axis=1, concat_axis=1, tiled=True)  45.3 us
    all_to_all x1, waiting for transfers between devices, run_steps(): lax.all_to_all(outgoing, 'ep', split_axis=1, concat_axis=1, tiled=True)  40.2 us
    unnamed x37, local copies, waits for them, and re-layouts  38.4 us
  transfers between devices with their start and end apart: 19, of which 14 were waited for; matrix products, arithmetic and copies ran while one was open for 25% of the time, Pallas kernels for 0%

profile of v1, /device:TPU:8, one launch (start us, length us, event | category | flops | bytes accessed | tf_op | source)
XLA Modules:
  0.0 793.0 jit_solution(11217073897088997112)
XLA Ops:
  9.0 9.0 %reduce-window.16 = s32[1,32,8,128]{3,2,1,0:T(8,128)S(1)} reduce-window(s32[1,32,8,128]{3,2,1,0:T(8,128)S(1)} %bitcast.249, s32[]{:T(128)} %constant.68.clone.1), window={size=1x1x1x128 pad=0_0x0_0x0_0x127_0}, to_apply=%region_7.9 | reduce-window | flops 4161536 | bytes 262148 | tf_op jit(solution)/shard_map/reduce-window.2
  18.4 9.0 %reduce-window.14 = s32[1,32,8,128]{3,2,1,0:T(8,128)S(1)} reduce-window(s32[1,32,8,128]{3,2,1,0:T(8,128)S(1)} %bitcast.250, s32[]{:T(128)} %constant.68.clone.1), window={size=1x1x1x128 pad=0_0x0_0x0_0x127_0}, to_apply=%region_1.2 | reduce-window | flops 4161536 | bytes 262148 | tf_op jit(solution)/shard_map/reduce-window
  31.4 64.7 %all_to_all.45 = bf16[1,8,160,1024]{3,2,0,1:T(8,128)(2,1)} all-to-all(bf16[1,8,160,1024]{3,2,0,1:T(8,128)(2,1)S(1)} %bitcast.246), channel_id=1, replica_groups=mesh['ep'=8,'tp'=4] {'ep'}, dimensions={1} | all-to-all | bytes 5242880 | tf_op jit(solution)/shard_map/all_to_all | solution.py:71
  108.5 6.8 constant_dynamic-slice_fusion
  121.5 40.2 %all-to-all-done = bf16[1,8,160,1024]{3,2,0,1:T(8,128)(2,1)} async-done(((bf16[1,8,160,1024]{3,2,0,1:T(8,128)(2,1)}), bf16[1,8,160,1024]{3,2,0,1:T(8,128)(2,1)}, u32[]{:S(2)}, u32[]{:S(2)}) %all-to-all-start) | async-done | bytes 2621472 | tf_op jit(solution)/shard_map/all_to_all | solution.py:71
  161.8 6.2 all-to-all-start.5
  178.0 58.4 %all-to-all-done.5 = bf16[384,8,512]{2,0,1:T(8,128)(2,1)S(1)} async-done(((bf16[384,8,512]{2,0,1:T(8,128)(2,1)}), bf16[384,8,512]{2,0,1:T(8,128)(2,1)S(1)}, u32[]{:S(2)}, u32[]{:S(2)}) %all-to-all-start.5) | async-done | bytes 3145760 | tf_op jit(solution)/shard_map/all_to_all | solution.py:116
  238.1 6.8 all-to-all-start.4
  254.6 58.0 %all-to-all-done.4 = bf16[384,8,512]{2,0,1:T(8,128)(2,1)} async-done(((bf16[384,8,512]{2,0,1:T(8,128)(2,1)}), bf16[384,8,512]{2,0,1:T(8,128)(2,1)}, u32[]{:S(2)}, u32[]{:S(2)}) %all-to-all-start.4) | async-done | bytes 3145760 | tf_op jit(solution)/shard_map/all_to_all | solution.py:115
  312.6 6.2 all-to-all-start.7
  327.4 6.2 select_bitcast_fusion
  333.6 53.7 %all-to-all-done.7 = bf16[1536,8,128]{2,0,1:T(8,128)(2,1)S(1)} async-done(((bf16[1536,8,128]{2,0,1:T(8,128)(2,1)}), bf16[1536,8,128]{2,0,1:T(8,128)(2,1)S(1)}, u32[]{:S(2)}, u32[]{:S(2)}) %all-to-all-start.7) | async-done | bytes 3145760 | tf_op jit(solution)/shard_map/all_to_all | solution.py:117
  395.5 15.1 %fusion.8 = f32[4,8,40,384]{3,2,1,0:T(8,128)} fusion(bf16[4,384,4096]{2,1,0:T(8,128)(2,1)} %param.15, bf16[8,4,40,4096]{3,2,1,0:T(8,128)(2,1)} %bitcast.257), kind=kOutput, calls=%fused_computation.14 | convolution fusion | flops 4026531840 | bytes 25034752 | tf_op jit(solution)/shard_map/bsecd,efd->bsecf/dot_general | solution.py:74
  410.6 15.3 %fusion.30 = bf16[1,8,4,40,384]{4,3,1,2,0:T(8,128)(2,1)} fusion(f32[4,8,40,384]{3,2,1,0:T(8,128)} %fusion.8, bf16[4,384,4096]{2,1,0:T(8,128)(2,1)} %param.16, bf16[8,4,40,4096]{3,2,1,0:T(8,128)(2,1)} %bitcast.258), kind=kOutput, calls=%fused_computation.42 | convolution fusion | flops 4029480960 | bytes 26017792 | tf_op jit(solution)/shard_map/bsecd,efd->bsecf/dot_general | solution.py:77
  434.3 29.1 %all-to-all-done.6 = bf16[384,8,512]{2,0,1:T(8,128)(2,1)S(1)} async-done(((bf16[384,8,512]{2,0,1:T(8,128)(2,1)}), bf16[384,8,512]{2,0,1:T(8,128)(2,1)S(1)}, u32[]{:S(2)}, u32[]{:S(2)}) %all-to-all-start.6) | async-done | bytes 3145760 | tf_op jit(solution)/shard_map/all_to_all | solution.py:124
  465.0 6.8 all-to-all-start.8
  472.0 14.2 %fusion.10 = f32[4,8,40,384]{3,2,1,0:T(8,128)S(1)} fusion(bf16[4,384,4096]{2,1,0:T(8,128)(2,1)} %param.15, bf16[8,4,40,4096]{3,2,1,0:T(8,128)(2,1)} %bitcast.259), kind=kOutput, calls=%fused_computation.16 | convolution fusion | flops 4026531840 | bytes 25034752 | tf_op jit(solution)/shard_map/bsecd,efd->bsecf/dot_general | solution.py:74
  486.2 15.0 %fusion.31 = bf16[1,8,4,40,384]{4,3,1,2,0:T(8,128)(2,1)} fusion(f32[4,8,40,384]{3,2,1,0:T(8,128)S(1)} %fusion.10, bf16[4,384,4096]{2,1,0:T(8,128)(2,1)} %param.16, bf16[8,4,40,4096]{3,2,1,0:T(8,128)(2,1)} %bitcast.260), kind=kOutput, calls=%fused_computation.44 | convolution fusion | flops 4029480960 | bytes 26017792 | tf_op jit(solution)/shard_map/bsecd,efd->bsecf/dot_general | solution.py:77
  501.3 10.0 %convert_bitcast_fusion = bf16[1,8,4,40,1024]{4,3,1,2,0:T(8,128)(2,1)S(1)} fusion(bf16[4,1536,1024]{2,1,0:T(8,128)(2,1)} %param.17, bf16[1,8,4,40,1536]{4,3,1,2,0:T(8,128)(2,1)} %all-gather.11.cloned.1.call-done), kind=kOutput, calls=%fused_computation.37 | convolution fusion | flops 4027842560 | bytes 19136512 | tf_op jit(solution)/shard_map/bsecf,efd->bsecd/dot_general | solution.py:81
  513.1 26.5 %all-to-all-done.8 = bf16[1536,8,128]{2,0,1:T(8,128)(2,1)} async-done(((bf16[1536,8,128]{2,0,1:T(8,128)(2,1)}), bf16[1536,8,128]{2,0,1:T(8,128)(2,1)}, u32[]{:S(2)}, u32[]{:S(2)}) %all-to-all-start.8) | async-done | bytes 3145760 | tf_op jit(solution)/shard_map/all_to_all | solution.py:125
  539.6 6.4 all-to-all-start.3
  546.0 10.0 %convert_bitcast_fusion.1 = bf16[1,8,4,40,1024]{4,3,1,2,0:T(8,128)(2,1)S(1)} fusion(bf16[4,1536,1024]{2,1,0:T(8,128)(2,1)} %param.17, bf16[1,8,4,40,1536]{4,3,1,2,0:T(8,128)(2,1)} %all-gather.7.cloned.1.call-done), kind=kOutput, calls=%fused_computation.38 | convolution fusion | flops 4027842560 | bytes 19136512 | tf_op jit(solution)/shard_map/bsecf,efd->bsecd/dot_general | solution.py:81
  557.8 45.3 %all-to-all-done.3 = bf16[1,8,160,1024]{3,2,0,1:T(8,128)(2,1)S(1)} async-done(((bf16[1,8,160,1024]{3,2,0,1:T(8,128)(2,1)}), bf16[1,8,160,1024]{3,2,0,1:T(8,128)(2,1)S(1)}, u32[]{:S(2)}, u32[]{:S(2)}) %all-to-all-start.3) | async-done | bytes 2621472 | tf_op jit(solution)/shard_map/all_to_all | solution.py:88
  603.2 6.7 all-to-all-start.1
  623.9 16.1 %collective-permute-done = bf16[384,1,512]{2,0,1:T(8,128)(2,1)} collective-permute-done((bf16[384,1,512]{2,0,1:T(8,128)(2,1)}, bf16[384,1,512]{2,0,1:T(8,128)(2,1)}, u32[]{:S(2)}, u32[]{:S(2)}) %collective-permute-start) | collective-permute-done | bytes 393248 | tf_op jit(solution)/shard_map/ppermute | solution.py:31
  640.0 6.4 collective-permute-start.5
  648.1 15.1 %collective-permute-done.1 = bf16[384,1,512]{2,0,1:T(8,128)(2,1)} collective-permute-done((bf16[384,1,512]{2,0,1:T(8,128)(2,1)}, bf16[384,1,512]{2,0,1:T(8,128)(2,1)}, u32[]{:S(2)}, u32[]{:S(2)}) %collective-permute-start.1) | collective-permute-done | bytes 393248 | tf_op jit(solution)/shard_map/ppermute | solution.py:31
  673.5 35.2 %collective-permute-done.3 = bf16[384,1,512]{2,0,1:T(8,128)(2,1)S(1)} collective-permute-done((bf16[384,1,512]{2,0,1:T(8,128)(2,1)}, bf16[384,1,512]{2,0,1:T(8,128)(2,1)S(1)}, u32[]{:S(2)}, u32[]{:S(2)}) %collective-permute-start.3) | collective-permute-done | bytes 393248 | tf_op jit(solution)/shard_map/ppermute | solution.py:31
  709.5 7.7 collective-permute-done.4
  717.9 10.4 %collective-permute-done.5 = bf16[384,1,512]{2,0,1:T(8,128)(2,1)S(1)} collective-permute-done((bf16[384,1,512]{2,0,1:T(8,128)(2,1)S(1)}, bf16[384,1,512]{2,0,1:T(8,128)(2,1)S(1)}, u32[]{:S(2)}, u32[]{:S(2)}) %collective-permute-start.5) | collective-permute-done | bytes 393248 | tf_op jit(solution)/shard_map/ppermute | solution.py:31
  729.1 6.7 collective-permute-done.6
  774.1 8.2 %gather_fusion.2 = bf16[1024,1024]{1,0:T(8,128)(2,1)} fusion(bf16[1280,1024]{1,0:T(8,128)(2,1)} %bitcast.32, s32[1024]{0:T(1024)S(1)} %broadcast_clamp_fusion.1), kind=kCustom, calls=%fused_computation.clone | custom fusion | bytes 4198400 | tf_op jit(solution)/shard_map/jit(take_along_axis)/gather | solution.py:91
  (135 shorter events, 145.3 us)
Async XLA Ops:
  7.2 23.3 %copy-start.5 = (bf16[2,128,1024]{2,1,0:T(8,128)(2,1)S(1)}, bf16[2,128,1024]{2,1,0:T(8,128)(2,1)}, u32[]{:S(2)}) copy-start(bf16[2,128,1024]{2,1,0:T(8,128)(2,1)} %param.12) | copy-start | bytes 1572868
  7.2 388.3 %all-gather.9.cloned.1.call-start = ((), (), s32[]{:S(2)}) async-start(), calls=%async_computation.11 | async-start | bytes 13107200 | tf_op jit(solution)/shard_map/all_gather | solution.py:72
  100.2 5.4 copy-start.9
  100.2 5.4 copy-start.10
  100.2 61.6 %all-to-all-start = ((bf16[1,8,160,1024]{3,2,0,1:T(8,128)(2,1)}), bf16[1,8,160,1024]{3,2,0,1:T(8,128)(2,1)}, u32[]{:S(2)}, u32[]{:S(2)}) async-start(bf16[1,8,160,1024]{3,2,0,1:T(8,128)(2,1)} %bitcast.8), calls=%async_computation | async-start | bytes 5242880 | tf_op jit(solution)/shard_map/all_to_all | solution.py:71
  161.8 74.6 %all-to-all-start.5 = ((bf16[384,8,512]{2,0,1:T(8,128)(2,1)}), bf16[384,8,512]{2,0,1:T(8,128)(2,1)S(1)}, u32[]{:S(2)}, u32[]{:S(2)}) async-start(bf16[384,8,512]{2,0,1:T(8,128)(2,1)} %copy.120), calls=%async_computation.5 | async-start | bytes 6291456 | tf_op jit(solution)/shard_map/all_to_all | solution.py:116
  168.0 304.1 %all-gather.5.cloned.1.call-start = ((), (), s32[]{:S(2)}) async-start(), calls=%async_computation.9 | async-start | bytes 13107200 | tf_op jit(solution)/shard_map/all_gather | solution.py:72
  236.4 1.7 copy-start.2
  238.1 74.5 %all-to-all-start.4 = ((bf16[384,8,512]{2,0,1:T(8,128)(2,1)}), bf16[384,8,512]{2,0,1:T(8,128)(2,1)}, u32[]{:S(2)}, u32[]{:S(2)}) async-start(bf16[384,8,512]{2,0,1:T(8,128)(2,1)} %copy.117), calls=%async_computation.4 | async-start | bytes 6291456 | tf_op jit(solution)/shard_map/all_to_all | solution.py:115
  312.6 74.6 %all-to-all-start.7 = ((bf16[1536,8,128]{2,0,1:T(8,128)(2,1)}), bf16[1536,8,128]{2,0,1:T(8,128)(2,1)S(1)}, u32[]{:S(2)}, u32[]{:S(2)}) async-start(bf16[1536,8,128]{2,0,1:T(8,128)(2,1)} %copy.123), calls=%async_computation.7 | async-start | bytes 6291456 | tf_op jit(solution)/shard_map/all_to_all | solution.py:117
  387.2 1.7 copy-start.1
  388.9 74.5 %all-to-all-start.6 = ((bf16[384,8,512]{2,0,1:T(8,128)(2,1)}), bf16[384,8,512]{2,0,1:T(8,128)(2,1)S(1)}, u32[]{:S(2)}, u32[]{:S(2)}) async-start(bf16[384,8,512]{2,0,1:T(8,128)(2,1)} %get-tuple-element.41), calls=%async_computation.6 | async-start | bytes 6291456 | tf_op jit(solution)/shard_map/all_to_all | solution.py:124
  395.0 106.3 %all-gather.11.cloned.1.call-start = ((), (), s32[]{:S(2)}) async-start(), calls=%async_computation.12 | async-start | bytes 4915200 | tf_op jit(solution)/shard_map/all_gather | solution.py:83
  463.4 1.6 copy-start
  465.0 74.5 %all-to-all-start.8 = ((bf16[1536,8,128]{2,0,1:T(8,128)(2,1)}), bf16[1536,8,128]{2,0,1:T(8,128)(2,1)}, u32[]{:S(2)}, u32[]{:S(2)}) async-start(bf16[1536,8,128]{2,0,1:T(8,128)(2,1)} %select_bitcast_fusion.2), calls=%async_computation.8 | async-start | bytes 6291456 | tf_op jit(solution)/shard_map/all_to_all | solution.py:125
  471.8 74.2 %all-gather.7.cloned.1.call-start = ((), (), s32[]{:S(2)}) async-start(), calls=%async_computation.10 | async-start | bytes 4915200 | tf_op jit(solution)/shard_map/all_gather | solution.py:83
  539.6 63.6 %all-to-all-start.3 = ((bf16[1,8,160,1024]{3,2,0,1:T(8,128)(2,1)}), bf16[1,8,160,1024]{3,2,0,1:T(8,128)(2,1)S(1)}, u32[]{:S(2)}, u32[]{:S(2)}) async-start(bf16[1,8,160,1024]{3,2,0,1:T(8,128)(2,1)} %bitcast.245), calls=%async_computation.3 | async-start | bytes 5242880 | tf_op jit(solution)/shard_map/all_to_all | solution.py:88
  557.8 53.0 %copy-start.6 = (f32[2,128,8]{1,2,0:T(8,128)S(1)}, f32[2,128,8]{1,2,0:T(8,128)}, u32[]{:S(2)}) copy-start(f32[2,128,8]{1,2,0:T(8,128)} %param.14) | copy-start | bytes 24580
  603.2 170.9 %all-to-all-start.1 = ((bf16[1,8,160,1024]{3,2,0,1:T(8,128)(2,1)}), bf16[1,8,160,1024]{3,2,0,1:T(8,128)(2,1)}, u32[]{:S(2)}, u32[]{:S(2)}) async-start(bf16[1,8,160,1024]{3,2,0,1:T(8,128)(2,1)} %bitcast.243), calls=%async_computation.1 | async-start | bytes 5242880 | tf_op jit(solution)/shard_map/all_to_all | solution.py:88
  614.5 25.5 %collective-permute-start = (bf16[384,1,512]{2,0,1:T(8,128)(2,1)}, bf16[384,1,512]{2,0,1:T(8,128)(2,1)}, u32[]{:S(2)}, u32[]{:S(2)}) collective-permute-start(bf16[384,1,512]{2,0,1:T(8,128)(2,1)} %get-tuple-element.32), channel_id=1, source_target_pairs={{0,4},{4,0},{8,12},{12,8},{16,20},{20,16},{24,28},{28,24},{1,5},{5... | collective-permute-start | bytes 1179656 | tf_op jit(solution)/shard_map/ppermute | solution.py:31
  616.0 47.3 %collective-permute-start.1 = (bf16[384,1,512]{2,0,1:T(8,128)(2,1)}, bf16[384,1,512]{2,0,1:T(8,128)(2,1)}, u32[]{:S(2)}, u32[]{:S(2)}) collective-permute-start(bf16[384,1,512]{2,0,1:T(8,128)(2,1)} %get-tuple-element.31), channel_id=1, source_target_pairs={{0,8},{4,12},{8,0},{12,4},{16,24},{20,28},{24,16},{28,20},{1,9},{5... | collective-permute-start | bytes 1179656 | tf_op jit(solution)/shard_map/ppermute | solution.py:31
  616.8 55.9 %collective-permute-start.2 = (bf16[384,1,512]{2,0,1:T(8,128)(2,1)}, bf16[384,1,512]{2,0,1:T(8,128)(2,1)S(1)}, u32[]{:S(2)}, u32[]{:S(2)}) collective-permute-start(bf16[384,1,512]{2,0,1:T(8,128)(2,1)} %get-tuple-element.30), channel_id=1, source_target_pairs={{0,12},{4,8},{8,4},{12,0},{16,28},{20,24},{24,20},{28,16},{1,13},{... | collective-permute-start | bytes 1179656 | tf_op jit(solution)/shard_map/ppermute | solution.py:31
  618.3 90.4 %collective-permute-start.3 = (bf16[384,1,512]{2,0,1:T(8,128)(2,1)}, bf16[384,1,512]{2,0,1:T(8,128)(2,1)S(1)}, u32[]{:S(2)}, u32[]{:S(2)}) collective-permute-start(bf16[384,1,512]{2,0,1:T(8,128)(2,1)} %get-tuple-element.29), channel_id=1, source_target_pairs={{0,16},{4,20},{8,24},{12,28},{16,0},{20,4},{24,8},{28,12},{1,17},{... | collective-permute-start | bytes 1179656 | tf_op jit(solution)/shard_map/ppermute | solution.py:31
  620.7 96.5 %collective-permute-start.4 = (bf16[384,1,512]{2,0,1:T(8,128)(2,1)}, bf16[384,1,512]{2,0,1:T(8,128)(2,1)S(1)}, u32[]{:S(2)}, u32[]{:S(2)}) collective-permute-start(bf16[384,1,512]{2,0,1:T(8,128)(2,1)} %get-tuple-element.28), channel_id=1, source_target_pairs={{0,20},{4,16},{8,28},{12,24},{16,4},{20,0},{24,12},{28,8},{1,21},{... | collective-permute-start | bytes 1179656 | tf_op jit(solution)/shard_map/ppermute | solution.py:31
  640.0 88.3 %collective-permute-start.5 = (bf16[384,1,512]{2,0,1:T(8,128)(2,1)S(1)}, bf16[384,1,512]{2,0,1:T(8,128)(2,1)S(1)}, u32[]{:S(2)}, u32[]{:S(2)}) collective-permute-start(bf16[384,1,512]{2,0,1:T(8,128)(2,1)S(1)} %get-tuple-element.27), channel_id=1, source_target_pairs={{0,24},{4,28},{8,16},{12,20},{16,8},{20,12},{24,0},{28,4},{1,25},{... | collective-permute-start | bytes 1179656 | tf_op jit(solution)/shard_map/ppermute | solution.py:31
  663.2 72.6 %collective-permute-start.6 = (bf16[384,1,512]{2,0,1:T(8,128)(2,1)S(1)}, bf16[384,1,512]{2,0,1:T(8,128)(2,1)S(1)}, u32[]{:S(2)}, u32[]{:S(2)}) collective-permute-start(bf16[384,1,512]{2,0,1:T(8,128)(2,1)S(1)} %get-tuple-element.26), channel_id=1, source_target_pairs={{0,28},{4,24},{8,20},{12,16},{16,12},{20,8},{24,4},{28,0},{1,29},{... | collective-permute-start | bytes 1179656 | tf_op jit(solution)/shard_map/ppermute | solution.py:31
  774.1 8.3 %copy-start.3 = (bf16[1024,1024]{1,0:T(8,128)(2,1)S(1)}, bf16[1024,1024]{1,0:T(8,128)(2,1)}, u32[]{:S(2)}) copy-start(bf16[1024,1024]{1,0:T(8,128)(2,1)} %gather_fusion.3) | copy-start | bytes 6291460
  774.1 8.3 %copy-start.7 = (pred[1024]{0:T(1024)(128)(4,1)S(1)}, pred[1024]{0:T(1024)(128)(4,1)}, u32[]{:S(2)}) copy-start(pred[1024]{0:T(1024)(128)(4,1)} %get-tuple-element.24) | copy-start | bytes 3076
  774.1 9.8 %copy-start.8 = (pred[1024]{0:T(1024)(128)(4,1)S(1)}, pred[1024]{0:T(1024)(128)(4,1)}, u32[]{:S(2)}) copy-start(pred[1024]{0:T(1024)(128)(4,1)} %get-tuple-element.22) | copy-start | bytes 3076
  782.3 1.6 copy-start.4
Sparse Core Ops, SparseCore 0:
  96.2 69.6 all-gather.8
  170.3 71.0 all-gather.4
  426.0 33.8 all-gather.10
  501.4 33.8 all-gather.6
